TPU v7x, 512 devices: a whole 4x8x8 slice. The times are simulated.
512 devices in a mesh: expert: 32 (over y, z_hi, core), tensor: 4 (over x), dp: 4 (over z_lo).
Axes of the slice: x: 4, y: 8, z: 8 (z_hi: 2, z_lo: 4; z = z_hi * 4 + z_lo), core: 2. Of those that a mesh axis runs over, the one named last changes fastest.
Arguments:
- tokens: bfloat16 [16384, 4096], P(('expert', 'dp'), 'tensor'), may hold values from -6 to 6
- routes: int32 [16384, 2], P(('expert', 'dp')), may hold values from 0 to 31, all different within a row; in each aligned block of 128 rows (0 to 127, 128 to 255, ...) at most 10 rows name the same one
- gate_prob: float32 [16384, 2], P(('expert', 'dp')), may hold values from 0.05 to 1
- token_count: int32 [128], P(('expert', 'dp')), may hold values from 1 to 128, 12288 in all
- gate_weight: bfloat16 [32, 4096, 1536], P(None, ('expert', 'dp'), 'tensor'), may hold values from -0.09375 to 0.09375
- up_weight: bfloat16 [32, 4096, 1536], P(None, ('expert', 'dp'), 'tensor'), may hold values from -0.09375 to 0.09375
- down_weight: bfloat16 [32, 4096, 1536], P(None, ('expert', 'dp'), 'tensor'), may hold values from -0.15625 to 0.15625
Outputs:
- mixed: bfloat16 [16384, 4096], P(('expert', 'dp'), 'tensor')
Inputs may be any that keep to these rules, and one draw needn't show every extreme that they name: `routes`: each row names 2 different experts; among the rows of one group (aligned blocks of 128 rows) no expert is named by more than 10 rows. `token_count`: rows of a group at or past its count are padding.
All inputs are finite; a program needn't handle non-finite values.
Results may differ from a plain program's by a relative error of at most 0.012.
Values may be sent and summed in bfloat16 or wider, within the bound.
A program may use at most 64 MiB of HBM per device.

v0:
```python
import jax
import jax.numpy as jnp
from jax import lax
from jax.sharding import PartitionSpec as P


def shards(tokens, routes, gate_prob, token_count, gate_weight, up_weight, down_weight):
    experts = gate_weight.shape[0]
    stored_rows = gate_weight.shape[1]
    hidden_share = gate_weight.shape[2]
    tok_rows, top_slots = routes.shape
    capacity = min(tok_rows, tok_rows * top_slots * 5 // (4 * experts))
    expert_count = lax.axis_size("expert")
    replica_count = lax.axis_size("dp")
    model_width = stored_rows * expert_count * replica_count
    arrived_rows = (
        lax.all_to_all(gate_weight, "expert", split_axis=0, concat_axis=1, tiled=True),
        lax.all_to_all(up_weight, "expert", split_axis=0, concat_axis=1, tiled=True),
        lax.all_to_all(down_weight, "expert", split_axis=0, concat_axis=1, tiled=True),
    )

    def split_blocks(weight):
        return weight.reshape(1, expert_count, 1, stored_rows, hidden_share)

    assembled = (
        lax.all_gather(split_blocks(arrived_rows[0]), "dp", axis=2, tiled=True),
        lax.all_gather(split_blocks(arrived_rows[1]), "dp", axis=2, tiled=True),
        lax.all_gather(split_blocks(arrived_rows[2]), "dp", axis=2, tiled=True),
    )
    w_gate = assembled[0].reshape(model_width, hidden_share)
    w_up = assembled[1].reshape(model_width, hidden_share)
    w_down = assembled[2].reshape(model_width, hidden_share)
    positions = jnp.arange(tok_rows)
    live_rows = positions < token_count[0]
    live_pair = jnp.repeat(live_rows, top_slots)
    route_flat = routes.reshape(-1)
    expert_ids = jnp.arange(experts)
    one_hot = ((route_flat[:, None] == expert_ids[None, :]) & live_pair[:, None]).astype(jnp.int32)
    pair_rank = jnp.sum((jnp.cumsum(one_hot, axis=0) - one_hot) * one_hot, axis=1)
    slot_of_pair = jnp.where(live_pair, route_flat * capacity + pair_rank, -1)
    slot_ids = jnp.arange(experts * capacity)
    assign_pair = (slot_ids[:, None] == slot_of_pair[None, :]).astype(jnp.bfloat16)
    assign_slots = assign_pair.reshape(experts * capacity, tok_rows, top_slots)
    assign_bf16 = jnp.sum(assign_slots.astype(jnp.float32), axis=2).astype(jnp.bfloat16)
    outgoing = jnp.dot(assign_bf16, tokens, preferred_element_type=jnp.float32).astype(jnp.bfloat16)
    incoming = lax.all_to_all(
        outgoing.reshape(experts, capacity, tokens.shape[1]),
        "expert",
        split_axis=0,
        concat_axis=0,
        tiled=True,
    )
    feature_piece = lax.all_gather(incoming, "tensor", axis=2, tiled=True)
    piece_width = feature_piece.shape[2]
    flat_piece = feature_piece.reshape(-1, piece_width)
    gate_proj = jnp.dot(flat_piece, w_gate, preferred_element_type=jnp.float32)
    up_proj = jnp.dot(flat_piece, w_up, preferred_element_type=jnp.float32)
    hidden = (jax.nn.silu(gate_proj) * up_proj).astype(jnp.bfloat16)
    partial_value = lax.dot_general(
        hidden, w_down, (((1,), (1,)), ((), ())), preferred_element_type=jnp.float32
    )
    expert_out = lax.psum_scatter(
        partial_value.astype(jnp.bfloat16), "tensor", scatter_dimension=1, tiled=True
    )
    returned = lax.all_to_all(
        expert_out.reshape(experts, capacity, -1), "expert", split_axis=0, concat_axis=0, tiled=True
    )
    returned_rows = returned.reshape(experts * capacity, -1)
    picked = jnp.einsum(
        "cts,cd->std", assign_slots, returned_rows, preferred_element_type=jnp.float32
    )
    slot_weights = gate_prob.T
    mixed = jnp.sum(slot_weights[:, :, None] * picked, axis=0)
    return mixed.astype(jnp.bfloat16)


def solution(mesh):
    in_specs = (
        P(("expert", "dp"), "tensor"),
        P(("expert", "dp"), None),
        P(("expert", "dp"), None),
        P(("expert", "dp")),
        P(None, ("expert", "dp"), "tensor"),
        P(None, ("expert", "dp"), "tensor"),
        P(None, ("expert", "dp"), "tensor"),
    )
    out_specs = P(("expert", "dp"), "tensor")
    return jax.shard_map(shards, mesh=mesh, in_specs=in_specs, out_specs=out_specs, check_vma=False)
```

profile of v0, /device:TPU:1, one launch (start us, length us, event | category | flops | bytes accessed | tf_op | source)
XLA Modules:
  0.0 439.4 jit_solution(14603103869681247513)
XLA Ops:
  6.5 0.8 copy.30
  7.4 0.1 eq.66
  7.5 0.1 eq.62
  8.3 0.1 broadcast_in_dim.16
  8.4 0.1 broadcast_in_dim.17
  8.6 0.6 reduce-window.6
  9.2 0.2 slice_reduce_fusion
  9.4 0.1 broadcast_in_dim.15.clone
  9.5 0.1 and.16
  9.7 0.1 fusion.16
  9.8 0.1 reduce_sum.33
  9.9 0.1 copy.34
  10.0 0.7 add_select_fusion
  10.7 0.3 convolution_convert_fusion.1
  11.1 0.2 reshape.115
  11.3 47.6 %all_to_all.37 = bf16[32,10,1024]{2,1,0:T(8,128)(2,1)} all-to-all(bf16[32,10,1024]{2,1,0:T(8,128)(2,1)S(1)} %reshape.115), channel_id=1, replica_groups=mesh['expert'=32,'tensor'=4,'dp'=4] {'expert'}, dimensions={0} | all-to-all | bytes 1310720 | tf_op jit(solution)/shard_map/all_to_all | solution.py:46
  59.0 31.1 %all_to_all.38 = bf16[32,32,384]{2,1,0:T(8,128)(2,1)} all-to-all(bf16[32,32,384]{2,1,0:T(8,128)(2,1)S(1)} %copy-done.1), channel_id=1, replica_groups=mesh['expert'=32,'tensor'=4,'dp'=4] {'expert'}, dimensions={0} | all-to-all | bytes 1572864 | tf_op jit(solution)/shard_map/all_to_all | solution.py:17
  90.1 30.9 %all_to_all.39 = bf16[32,32,384]{2,1,0:T(8,128)(2,1)} all-to-all(bf16[32,32,384]{2,1,0:T(8,128)(2,1)S(1)} %copy-done.2), channel_id=1, replica_groups=mesh['expert'=32,'tensor'=4,'dp'=4] {'expert'}, dimensions={0} | all-to-all | bytes 1572864 | tf_op jit(solution)/shard_map/all_to_all | solution.py:18
  121.0 30.7 %all_to_all.40 = bf16[32,32,384]{2,1,0:T(8,128)(2,1)} all-to-all(bf16[32,32,384]{2,1,0:T(8,128)(2,1)S(1)} %copy-done.3), channel_id=1, replica_groups=mesh['expert'=32,'tensor'=4,'dp'=4] {'expert'}, dimensions={0} | all-to-all | bytes 1572864 | tf_op jit(solution)/shard_map/all_to_all | solution.py:19
  151.8 0.0 reduce-scatter.2.cloned.1.call-start
  151.9 3.3 reshape.116
  155.2 41.5 %all-gather.10.cloned.1.call-done = bf16[32,128,384]{2,1,0:T(8,128)(2,1)} async-done(((bf16[32,32,384]{2,1,0:T(8,128)(2,1)}), bf16[32,128,384]{2,1,0:T(8,128)(2,1)}) %all-gather.10.cloned.1.call-update) | async-done | bytes 3145744 | tf_op jit(solution)/shard_map/all_gather | solution.py:26
  196.7 3.4 fusion.21
  200.1 68.5 %all-gather.12.cloned.1.call-done = bf16[32,128,384]{2,1,0:T(8,128)(2,1)} async-done(((bf16[32,32,384]{2,1,0:T(8,128)(2,1)}), bf16[32,128,384]{2,1,0:T(8,128)(2,1)}) %all-gather.12.cloned.1.call-update) | async-done | bytes 3145744 | tf_op jit(solution)/shard_map/all_gather | solution.py:27
  268.7 71.8 %all-gather.14.cloned.1.call-done = bf16[32,128,384]{2,1,0:T(8,128)(2,1)} async-done(((bf16[32,32,384]{2,1,0:T(8,128)(2,1)}), bf16[32,128,384]{2,1,0:T(8,128)(2,1)}) %all-gather.14.cloned.1.call-update) | async-done | bytes 3145744 | tf_op jit(solution)/shard_map/all_gather | solution.py:28
  340.5 7.3 %convolution_convert_fusion = bf16[320,4096]{1,0:T(8,128)(2,1)} fusion(bf16[4096,384]{1,0:T(8,128)(2,1)} %bitcast.45, bf16[320,4096]{1,0:T(8,128)(2,1)S(1)} %reshape.116, bf16[4096,384]{1,0:T(8,128)(2,1)} %bitcast.44, f32[320,384]{1,0:T(8,128)S(1)} %fusion.21), kind=kOutput, calls=%fused_computation | convolution fusion | flops 2015313920 | bytes 12025856 | tf_op jit(solution)/shard_map/dot_general | solution.py:59
  347.8 39.7 %reduce-scatter.2.cloned.1.call-done = bf16[320,1024]{1,0:T(8,128)(2,1)} async-done(((bf16[320,4096]{1,0:T(8,128)(2,1)}), bf16[320,1024]{1,0:T(8,128)(2,1)}) %reduce-scatter.2.cloned.1.call-update) | async-done | bytes 655376 | tf_op jit(solution)/shard_map/reduce_scatter | solution.py:62
  387.5 1.3 reshape.123
  388.8 42.5 %all_to_all.41 = bf16[32,10,1024]{2,1,0:T(8,128)(2,1)S(1)} all-to-all(bf16[32,10,1024]{2,1,0:T(8,128)(2,1)S(1)} %reshape.123), channel_id=1, replica_groups=mesh['expert'=32,'tensor'=4,'dp'=4] {'expert'}, dimensions={0} | all-to-all | bytes 1310720 | tf_op jit(solution)/shard_map/all_to_all | solution.py:65
  431.3 0.2 reshape.131
  431.5 0.5 fusion.1
  432.0 0.9 copy.35
  (26 shorter events, 0.4 us)
Async XLA Ops:
  6.5 4.2 copy-start
  6.5 145.3 %all-gather.8.cloned.1.call-start = ((), (), s32[]{:S(2)}) async-start(), calls=%async_computation.6 | async-start | bytes 5242880 | tf_op jit(solution)/shard_map/all_gather | solution.py:53
  8.6 50.4 %copy-start.1 = (bf16[32,32,384]{2,1,0:T(8,128)(2,1)S(1)}, bf16[32,32,384]{2,1,0:T(8,128)(2,1)}, u32[]{:S(2)}) copy-start(bf16[32,32,384]{2,1,0:T(8,128)(2,1)} %param.11) | copy-start | bytes 2359300
  11.3 78.8 %copy-start.2 = (bf16[32,32,384]{2,1,0:T(8,128)(2,1)S(1)}, bf16[32,32,384]{2,1,0:T(8,128)(2,1)}, u32[]{:S(2)}) copy-start(bf16[32,32,384]{2,1,0:T(8,128)(2,1)} %param.12) | copy-start | bytes 2359300
  58.9 62.2 %copy-start.3 = (bf16[32,32,384]{2,1,0:T(8,128)(2,1)S(1)}, bf16[32,32,384]{2,1,0:T(8,128)(2,1)}, u32[]{:S(2)}) copy-start(bf16[32,32,384]{2,1,0:T(8,128)(2,1)} %param.13) | copy-start | bytes 2359300
  58.9 137.8 %all-gather.10.cloned.1.call-start = ((), (), s32[]{:S(2)}) async-start(), calls=%async_computation.8 | async-start | bytes 3932160 | tf_op jit(solution)/shard_map/all_gather | solution.py:26
  90.0 178.6 %all-gather.12.cloned.1.call-start = ((), (), s32[]{:S(2)}) async-start(), calls=%async_computation.9 | async-start | bytes 3932160 | tf_op jit(solution)/shard_map/all_gather | solution.py:27
  121.0 219.5 %all-gather.14.cloned.1.call-start = ((), (), s32[]{:S(2)}) async-start(), calls=%async_computation.10 | async-start | bytes 3932160 | tf_op jit(solution)/shard_map/all_gather | solution.py:28
  151.8 235.7 %reduce-scatter.2.cloned.1.call-start = ((), (), s32[]{:S(2)}) async-start(), calls=%async_computation.7 | async-start | bytes 3276800 | tf_op jit(solution)/shard_map/reduce_scatter | solution.py:62
  347.8 83.7 %copy-start.4 = (f32[128,2]{0,1:T(2,128)S(1)}, f32[128,2]{0,1:T(2,128)}, u32[]{:S(2)}) copy-start(f32[128,2]{0,1:T(2,128)} %param.9) | copy-start | bytes 3076
Sparse Core Ops, SparseCore 0:
  59.0 49.7 all-gather.7
  110.9 85.8 all-gather.9
  198.8 69.7 all-gather.11
  270.6 69.7 all-gather.13
  347.9 39.5 reduce-scatter.1
where the time goes:
time: 440 us; the launch traced here: 439 us
  waiting for transfers between devices  222 us (50%)
  blocking collectives  183 us (42%)
  between operations  14 us (3%)
  matrix products  11.5 us (3%)
  local copies, waits for them, and re-layouts  7.87 us (2%)
    all_gather x1, waiting for transfers between devices, shards(): lax.all_gather(split_blocks(arrived_rows[2]), 'dp', axis=2, tiled=True)  71.8 us
    all_gather x1, waiting for transfers between devices, shards(): lax.all_gather(split_blocks(arrived_rows[1]), 'dp', axis=2, tiled=True)  68.5 us
    all_to_all x1, blocking collectives, shards(): lax.all_to_all(outgoing.reshape(experts, capacity, tokens.shape[1]), 'exp...  47.6 us
    all_to_all x1, blocking collectives, shards(): lax.all_to_all(expert_out.reshape(experts, capacity, -1), 'expert', split...  42.5 us
    all_gather x1, waiting for transfers between devices, shards(): lax.all_gather(split_blocks(arrived_rows[0]), 'dp', axis=2, tiled=True)  41.5 us
    reduce_scatter x1, waiting for transfers between devices, shards(): lax.psum_scatter(partial_value.astype(jnp.bfloat16), 'tensor', scatter_di...  39.7 us
    all_to_all x1, blocking collectives, shards(): lax.all_to_all(gate_weight, 'expert', split_axis=0, concat_axis=1, tiled=...  31.1 us
    all_to_all x1, blocking collectives, shards(): lax.all_to_all(up_weight, 'expert', split_axis=0, concat_axis=1, tiled=True)  30.9 us
  transfers between devices with their start and end apart: 5, of which 4 were waited for; matrix products, arithmetic and copies ran while one was open for 2% of the time, Pallas kernels for 0%

commit v1 on v0

--- a/solution.py
+++ b/solution.py
@@ -23,7 +23,12 @@
         return weight.reshape(1, expert_count, 1, stored_rows, hidden_share)
 
     assembled = (
-        lax.all_gather(split_blocks(arrived_rows[0]), "dp", axis=2, tiled=True),
+        jnp.concatenate(
+            lax.all_to_all(
+                jnp.stack([split_blocks(arrived_rows[0])] * lax.axis_size("dp")), "dp", 0, 0
+            ),
+            axis=2,
+        ),
         lax.all_gather(split_blocks(arrived_rows[1]), "dp", axis=2, tiled=True),
         lax.all_gather(split_blocks(arrived_rows[2]), "dp", axis=2, tiled=True),
     )

time: 440 us -> 421 us (0.957)
  waiting for transfers between devices: 222 us -> 196 us
  local copies, waits for them, and re-layouts: 7.87 us -> 13.1 us
    all_to_all x0 -> x1, waiting for transfers between devices: none -> 102 us  [shards(): lax.all_to_all(jnp.stack([split_blocks(arrived_rows[0])] * lax.axis_size(...]
    all_gather x1, waiting for transfers between devices: 68.5 us -> 0.02 us  [shards(): lax.all_gather(split_blocks(arrived_rows[1]), 'dp', axis=2, tiled=True)]
    all_gather x1 -> x0, waiting for transfers between devices: 41.5 us -> none  [shards(): lax.all_gather(split_blocks(arrived_rows[0]), 'dp', axis=2, tiled=True)]
    all_gather x1, waiting for transfers between devices: 71.8 us -> 53.2 us  [shards(): lax.all_gather(split_blocks(arrived_rows[2]), 'dp', axis=2, tiled=True)]
  transfers between devices with their start and end apart: 5 -> 5, of which waited for: 4 -> 3; matrix products, arithmetic and copies ran while one was open for 2% -> 2% of each run, Pallas kernels for 0% -> 0%
where the time goes in v1:
time: 421 us
  waiting for transfers between devices  196 us (47%)
  blocking collectives  183 us (43%)
  between operations  14 us (3%)
  local copies, waits for them, and re-layouts  13.1 us (3%)
  matrix products  9.65 us (2%)
    all_to_all x1, waiting for transfers between devices, shards(): lax.all_to_all(jnp.stack([split_blocks(arrived_rows[0])] * lax.axis_size(...  102 us
    all_gather x1, waiting for transfers between devices, shards(): lax.all_gather(split_blocks(arrived_rows[2]), 'dp', axis=2, tiled=True)  53.2 us
    all_to_all x1, blocking collectives, shards(): lax.all_to_all(outgoing.reshape(experts, capacity, tokens.shape[1]), 'exp...  47.6 us
    all_to_all x1, blocking collectives, shards(): lax.all_to_all(expert_out.reshape(experts, capacity, -1), 'expert', split...  42.5 us
    reduce_scatter x1, waiting for transfers between devices, shards(): lax.psum_scatter(partial_value.astype(jnp.bfloat16), 'tensor', scatter_di...  39.7 us
    all_to_all x1, blocking collectives, shards(): lax.all_to_all(up_weight, 'expert', split_axis=0, concat_axis=1, tiled=True)  31.1 us
    all_to_all x1, blocking collectives, shards(): lax.all_to_all(gate_weight, 'expert', split_axis=0, concat_axis=1, tiled=...  30.8 us
    all_to_all x1, blocking collectives, shards(): lax.all_to_all(down_weight, 'expert', split_axis=0, concat_axis=1, tiled=...  30.7 us
  transfers between devices with their start and end apart: 5, of which 3 were waited for; matrix products, arithmetic and copies ran while one was open for 2% of the time, Pallas kernels for 0%

profile of v1, /device:TPU:1, one launch (start us, length us, event | category | flops | bytes accessed | tf_op | source)
XLA Modules:
  0.0 420.8 jit_solution(10964825765243975783)
XLA Ops:
  6.5 0.8 copy.32
  7.4 0.1 eq.66
  7.5 0.1 eq.62
  8.4 0.1 broadcast_in_dim.17
  8.6 0.6 reduce-window.6
  9.2 0.2 slice_reduce_fusion
  9.5 0.1 and.16
  9.7 0.1 fusion.16
  9.8 0.1 reduce_sum.33
  10.0 0.7 add_select_fusion
  10.7 0.3 convolution_convert_fusion.1
  11.1 0.2 reshape.114
  11.3 47.6 %all_to_all.42 = bf16[32,10,1024]{2,1,0:T(8,128)(2,1)} all-to-all(bf16[32,10,1024]{2,1,0:T(8,128)(2,1)S(1)} %reshape.114), channel_id=1, replica_groups=mesh['expert'=32,'tensor'=4,'dp'=4] {'expert'}, dimensions={0} | all-to-all | bytes 1310720 | tf_op jit(solution)/shard_map/all_to_all | solution.py:51
  59.0 31.1 %all_to_all.43 = bf16[32,32,384]{2,1,0:T(8,128)(2,1)} all-to-all(bf16[32,32,384]{2,1,0:T(8,128)(2,1)S(1)} %copy-done.3), channel_id=1, replica_groups=mesh['expert'=32,'tensor'=4,'dp'=4] {'expert'}, dimensions={0} | all-to-all | bytes 1572864 | tf_op jit(solution)/shard_map/all_to_all | solution.py:18
  90.1 30.8 %all_to_all.44 = bf16[32,32,384]{2,1,0:T(8,128)(2,1)S(1)} all-to-all(bf16[32,32,384]{2,1,0:T(8,128)(2,1)S(1)} %copy-done.4), channel_id=1, replica_groups=mesh['expert'=32,'tensor'=4,'dp'=4] {'expert'}, dimensions={0} | all-to-all | bytes 1572864 | tf_op jit(solution)/shard_map/all_to_all | solution.py:17
  120.8 30.7 %all_to_all.45 = bf16[32,32,384]{2,1,0:T(8,128)(2,1)} all-to-all(bf16[32,32,384]{2,1,0:T(8,128)(2,1)S(1)} %copy-done.5), channel_id=1, replica_groups=mesh['expert'=32,'tensor'=4,'dp'=4] {'expert'}, dimensions={0} | all-to-all | bytes 1572864 | tf_op jit(solution)/shard_map/all_to_all | solution.py:19
  151.5 2.1 stack.3
  153.6 3.7 all-to-all-start.2
  157.3 0.7 all-gather.10.cloned.1.call-update
  158.1 4.7 %reshape.115 = bf16[320,4096]{1,0:T(8,128)(2,1)} reshape(bf16[32,10,4096]{2,1,0:T(8,128)(2,1)} %all-gather.6.cloned.1.call-done) | data formatting | bytes 5242880 | tf_op jit(solution)/shard_map/reshape | solution.py:60
  162.8 102.4 %all-to-all-done.2 = bf16[4,1,32,1,32,384]{5,4,2,3,1,0:T(8,128)(2,1)S(1)} async-done(((bf16[4,1,32,1,32,384]{5,4,2,3,1,0:T(8,128)(2,1)}), bf16[4,1,32,1,32,384]{5,4,2,3,1,0:T(8,128)(2,1)S(1)}, u32[]{:S(2)}, u32[]{:S(2)}) %all-to-all-start.2) | async-done | bytes 3145760 | tf_op jit(solution)/shard_map/all_to_all | solution.py:27
  265.2 0.6 copy.37
  265.8 1.3 copy-done.1
  267.0 1.5 fusion.21
  268.6 53.2 %all-gather.10.cloned.1.call-done = bf16[32,128,384]{2,1,0:T(8,128)(2,1)} async-done(((bf16[32,32,384]{2,1,0:T(8,128)(2,1)}), bf16[32,128,384]{2,1,0:T(8,128)(2,1)}) %all-gather.10.cloned.1.call-update) | async-done | bytes 3145744 | tf_op jit(solution)/shard_map/all_gather | solution.py:33
  321.8 7.3 %convolution_convert_fusion = bf16[320,4096]{1,0:T(8,128)(2,1)} fusion(bf16[4096,384]{1,0:T(8,128)(2,1)} %bitcast.47, bf16[320,4096]{1,0:T(8,128)(2,1)S(1)} %copy-done.2, bf16[4096,384]{1,0:T(8,128)(2,1)} %bitcast.46, f32[320,384]{1,0:T(8,128)S(1)} %fusion.21), kind=kOutput, calls=%fused_computation | convolution fusion | flops 2015313920 | bytes 12025856 | tf_op jit(solution)/shard_map/dot_general | solution.py:64
  329.2 39.7 %reduce-scatter.2.cloned.1.call-done = bf16[320,1024]{1,0:T(8,128)(2,1)} async-done(((bf16[320,4096]{1,0:T(8,128)(2,1)}), bf16[320,1024]{1,0:T(8,128)(2,1)}) %reduce-scatter.2.cloned.1.call-update) | async-done | bytes 655376 | tf_op jit(solution)/shard_map/reduce_scatter | solution.py:67
  368.9 1.3 reshape.121
  370.2 42.5 %all_to_all.46 = bf16[32,10,1024]{2,1,0:T(8,128)(2,1)S(1)} all-to-all(bf16[32,10,1024]{2,1,0:T(8,128)(2,1)S(1)} %reshape.121), channel_id=1, replica_groups=mesh['expert'=32,'tensor'=4,'dp'=4] {'expert'}, dimensions={0} | all-to-all | bytes 1310720 | tf_op jit(solution)/shard_map/all_to_all | solution.py:70
  412.7 0.2 reshape.127
  412.9 0.5 fusion.1
  413.4 0.9 copy.38
  (31 shorter events, 0.6 us)
Async XLA Ops:
  6.5 4.2 copy-start
  6.5 151.5 %all-gather.6.cloned.1.call-start = ((), (), s32[]{:S(2)}) async-start(), calls=%async_computation.7 | async-start | bytes 5242880 | tf_op jit(solution)/shard_map/all_gather | solution.py:58
  8.6 50.4 %copy-start.3 = (bf16[32,32,384]{2,1,0:T(8,128)(2,1)S(1)}, bf16[32,32,384]{2,1,0:T(8,128)(2,1)}, u32[]{:S(2)}) copy-start(bf16[32,32,384]{2,1,0:T(8,128)(2,1)} %param.12) | copy-start | bytes 2359300
  11.3 78.8 %copy-start.4 = (bf16[32,32,384]{2,1,0:T(8,128)(2,1)S(1)}, bf16[32,32,384]{2,1,0:T(8,128)(2,1)}, u32[]{:S(2)}) copy-start(bf16[32,32,384]{2,1,0:T(8,128)(2,1)} %param.11) | copy-start | bytes 2359300
  58.9 62.0 %copy-start.5 = (bf16[32,32,384]{2,1,0:T(8,128)(2,1)S(1)}, bf16[32,32,384]{2,1,0:T(8,128)(2,1)}, u32[]{:S(2)}) copy-start(bf16[32,32,384]{2,1,0:T(8,128)(2,1)} %param.13) | copy-start | bytes 2359300
  58.9 209.7 %all-gather.8.cloned.1.call-start = ((), (), s32[]{:S(2)}) async-start(), calls=%async_computation.9 | async-start | bytes 3932160 | tf_op jit(solution)/shard_map/all_gather | solution.py:32
  153.6 111.6 %all-to-all-start.2 = ((bf16[4,1,32,1,32,384]{5,4,2,3,1,0:T(8,128)(2,1)}), bf16[4,1,32,1,32,384]{5,4,2,3,1,0:T(8,128)(2,1)S(1)}, u32[]{:S(2)}, u32[]{:S(2)}) async-start(bf16[4,1,32,1,32,384]{5,4,2,3,1,0:T(8,128)(2,1)} %stack.3), calls=%async_computation.2 | async-start | bytes 6291456 | tf_op jit(solution)/shard_map/all_to_all | solution.py:27
  157.3 164.5 %all-gather.10.cloned.1.call-start = ((), (), s32[]{:S(2)}) async-start(), calls=%async_computation.10 | async-start | bytes 3932160 | tf_op jit(solution)/shard_map/all_gather | solution.py:33
  158.0 210.9 %reduce-scatter.2.cloned.1.call-start = ((), (), s32[]{:S(2)}) async-start(), calls=%async_computation.8 | async-start | bytes 3276800 | tf_op jit(solution)/shard_map/reduce_scatter | solution.py:67
  265.2 1.9 copy-start.1
  267.0 54.8 %copy-start.2 = (bf16[320,4096]{1,0:T(8,128)(2,1)S(1)}, bf16[320,4096]{1,0:T(8,128)(2,1)}, u32[]{:S(2)}) copy-start(bf16[320,4096]{1,0:T(8,128)(2,1)} %reshape.115) | copy-start | bytes 7864324
  329.2 83.8 %copy-start.6 = (f32[128,2]{0,1:T(2,128)S(1)}, f32[128,2]{0,1:T(2,128)}, u32[]{:S(2)}) copy-start(f32[128,2]{0,1:T(2,128)} %param.9) | copy-start | bytes 3076
Sparse Core Ops, SparseCore 0:
  59.0 49.7 all-gather.5
  110.9 119.3 all-gather.7
  232.3 89.4 all-gather.9
  329.3 39.5 reduce-scatter.1
